TPU v7x, 256 devices: a whole 4x4x8 slice. The times are simulated.
256 devices in a mesh: section: 4 (over x), dp: 4 (over y), chan: 16 (over z, core).
Axes of the slice: x: 4, y: 4, z: 8, core: 2. Of those that a mesh axis runs over, the one named last changes fastest.
Arguments:
- feats: bfloat16 [8, 32, 128, 2048], P('dp', None, None, 'chan'), may hold values from -6 to 6
- offsets: int32 [8], P('dp'), may hold values from 0 to 127
- widths: int32 [8], P('dp'), may hold values from 32 to 64
- labels: int32 [8, 32, 128], P('dp'), may hold values from 0 to 19
- dw_kernel: bfloat16 [4, 9, 2048], P('section', None, 'chan'), may hold values from -2 to 2
- pw_weight: bfloat16 [4, 2048, 256], P('section', 'chan'), may hold values from -0.125 to 0.125
- pw_bias: float32 [4, 256], P('section', 'chan'), may hold values from -3 to 3
- proj: bfloat16 [4, 256, 256], P('section', 'chan'), may hold values from -0.1875 to 0.1875
- proj_bias: float32 [256], P('chan'), may hold values from -3 to 3
- upstream: bfloat16 [256, 8, 32, 128], P('chan', 'dp'), may hold values from -6 to 6
Outputs:
- aspp_out: bfloat16 [256, 8, 32, 128], P('chan', 'dp')
- input_grad: bfloat16 [8, 32, 128, 2048], P('dp', 'section', None, 'chan')
- grad_dw: float32 [4, 9, 2048], P('section', None, 'chan')
- grad_pw: float32 [4, 2048, 256], P('section', 'chan')
- grad_pw_bias: float32 [4, 256], P('section', 'chan')
- grad_proj: float32 [4, 256, 256], P('section', 'chan')
- grad_proj_bias: float32 [256], P('chan')
All inputs are finite; a program needn't handle non-finite values.
Results may differ from a plain program's by a relative error of at most 0.008.
Values may be sent and summed in bfloat16 or wider, within the bound.
No kernel may reach another device: no remote copies, remote signals or barrier semaphores. Data moves between devices by JAX's collectives and lax.ppermute only.
A program may use at most 128 MiB of HBM per device.

v0:
```python
import math
import jax
import jax.numpy as jnp
from jax import lax
from jax.sharding import PartitionSpec as P

RATE = 6
void_class = 19


def prefix(shard, axis, combine, identity):
    devices, place = (lax.axis_size(axis), lax.axis_index(axis))
    everything = lax.all_gather(shard, axis)
    start = jnp.broadcast_to(jnp.asarray(identity, shard.dtype), shard.shape)

    def step(k, before):
        reached = k < place
        new = combine(before, everything[k])
        return jnp.where(reached, new, before)

    return lax.fori_loop(0, devices, step, start)


def spread(value, axis, source):
    kept = jnp.where(lax.axis_index(axis) == source, value, 0).astype(value.dtype)
    return lax.psum(kept, axis)


def column_band(offsets, widths, col_count):
    columns = jnp.arange(col_count, dtype=jnp.int32)
    return jnp.mod(columns[None, :] - offsets[:, None], col_count) < widths[:, None]


def swish_slope(value):
    sig = jax.nn.sigmoid(value)
    return sig * (1.0 + value * (1.0 - sig))


def add_terms(earlier, latter):
    return earlier + latter


def local(feats, offsets, widths, labels, dw_kernel, pw_weight, pw_bias, proj, proj_bias, upstream):
    frame_count, row_count, col_count, chan_count = feats.shape
    segments = lax.axis_size("section")
    dilation = RATE * lax.axis_index("section")
    margin = RATE * (segments - 1)
    keep = column_band(offsets, widths, col_count)
    masked = feats * keep[:, None, :, None].astype(jnp.bfloat16)
    padded = jnp.pad(masked, ((0, 0), (margin, margin), (margin, margin), (0, 0)))
    kernel = dw_kernel[0].astype(jnp.float32)
    pixel_count = frame_count * row_count * col_count
    scaling = 1.0 / math.sqrt(pixel_count * lax.axis_size("dp"))

    def tap_slice(source, tap_index, direction):
        row_step = tap_index // 3 - 1
        col_step = tap_index % 3 - 1
        anchor = (
            0,
            margin + direction * dilation * row_step,
            margin + direction * dilation * col_step,
            0,
        )
        return lax.dynamic_slice(source, anchor, (frame_count, row_count, col_count, chan_count))

    accum = jnp.zeros((frame_count, row_count, col_count, chan_count), jnp.float32)
    for tap_index in range(9):
        accum = accum + tap_slice(padded, tap_index, 1).astype(jnp.float32) * kernel[tap_index]
    depth_out = accum.astype(jnp.bfloat16)
    depth_rows = depth_out.reshape(pixel_count, chan_count)
    weight = pw_weight[0]
    branch_share = pw_bias.shape[1]
    columns = weight
    preact = (
        lax.psum_scatter(
            lax.dot_general(
                columns, depth_rows, (((0,), (1,)), ((), ())), preferred_element_type=jnp.float32
            ),
            "chan",
            scatter_dimension=0,
            tiled=True,
        )
        + pw_bias[0][:, None]
    )
    branch_act = jax.nn.silu(preact).astype(jnp.bfloat16)
    proj_local = proj[0]
    columns = proj_local
    zpart = lax.psum_scatter(
        lax.dot_general(
            columns, branch_act, (((0,), (0,)), ((), ())), preferred_element_type=jnp.float32
        ),
        "chan",
        scatter_dimension=0,
        tiled=True,
    )
    up_rows = upstream.reshape(branch_share, pixel_count).astype(jnp.float32)
    labeled = (labels != void_class).reshape(pixel_count).astype(jnp.float32)
    before = prefix(zpart, "section", add_terms, jnp.zeros_like(zpart))
    zvalue = before + zpart + proj_bias[:, None]
    result = jax.nn.silu(zvalue).astype(jnp.bfloat16)
    gradient = (up_rows * swish_slope(zvalue) * labeled[None, :]).astype(jnp.bfloat16)
    result, out_grad = (result, gradient)
    result, out_grad = (
        spread(result, "section", segments - 1),
        spread(out_grad, "section", segments - 1),
    )
    proj_bias_grad = jnp.sum(out_grad.astype(jnp.float32), axis=1) * scaling
    shard_rows = lax.all_gather(out_grad, "chan", axis=0, tiled=True)
    act_grad = jnp.dot(proj_local, shard_rows, preferred_element_type=jnp.float32)
    piece_grad = lax.dot_general(
        branch_act, shard_rows, (((1,), (1,)), ((), ())), preferred_element_type=jnp.float32
    )
    proj_grad = piece_grad
    act_grad, proj_grad = (act_grad, proj_grad)
    pre_grad = (act_grad * swish_slope(preact)).astype(jnp.bfloat16)
    pw_bias_grad = jnp.sum(pre_grad.astype(jnp.float32), axis=1) * scaling
    shard_rows = lax.all_gather(pre_grad, "chan", axis=0, tiled=True)
    columns = weight
    depth_acc = lax.dot_general(
        shard_rows, columns, (((0,), (1,)), ((), ())), preferred_element_type=jnp.float32
    )
    piece_grad = lax.dot_general(
        depth_rows, shard_rows, (((0,), (1,)), ((), ())), preferred_element_type=jnp.float32
    )
    weight_grad = piece_grad
    depth_acc, weight_grad = (depth_acc, weight_grad)
    depth_grad = depth_acc.astype(jnp.bfloat16).reshape(
        frame_count, row_count, col_count, chan_count
    )
    padded_grad = jnp.pad(depth_grad, ((0, 0), (margin, margin), (margin, margin), (0, 0)))
    depth_f = depth_grad.astype(jnp.float32)
    input_term = jnp.zeros((frame_count, row_count, col_count, chan_count), jnp.float32)
    tap_grads = []
    for tap_index in range(9):
        source = tap_slice(padded, tap_index, 1).astype(jnp.float32)
        tap_grads.append(jnp.sum(source * depth_f, axis=(0, 1, 2)) * scaling)
        input_term = (
            input_term
            + tap_slice(padded_grad, tap_index, -1).astype(jnp.float32) * kernel[tap_index]
        )
    kernel_grad = jnp.stack(tap_grads)
    input_rows = lax.psum_scatter(input_term, "section", scatter_dimension=1, tiled=True)
    input_grad = (input_rows * keep[:, None, :, None].astype(jnp.float32)).astype(jnp.bfloat16)
    kernel_grad, weight_grad, pw_bias_grad, proj_grad, proj_bias_grad = lax.psum(
        (kernel_grad, weight_grad * scaling, pw_bias_grad, proj_grad * scaling, proj_bias_grad),
        "dp",
    )
    aspp_out = result.reshape(branch_share, frame_count, row_count, col_count)
    return (
        aspp_out,
        input_grad,
        kernel_grad[None],
        weight_grad[None],
        pw_bias_grad[None],
        proj_grad[None],
        proj_bias_grad,
    )


def solution(mesh):
    in_specs = (
        P("dp", None, None, "chan"),
        P("dp"),
        P("dp"),
        P("dp", None, None),
        P("section", None, "chan"),
        P("section", "chan", None),
        P("section", "chan"),
        P("section", "chan", None),
        P("chan"),
        P("chan", "dp", None, None),
    )
    out_specs = (
        P("chan", "dp", None, None),
        P("dp", "section", None, "chan"),
        P("section", None, "chan"),
        P("section", "chan", None),
        P("section", "chan"),
        P("section", "chan", None),
        P("chan"),
    )
    return jax.shard_map(local, mesh=mesh, in_specs=in_specs, out_specs=out_specs, check_vma=False)
```

profile of v0, /device:TPU:2, one launch (start us, length us, event | category | flops | bytes accessed | tf_op | source)
XLA Modules:
  0.0 520.5 jit_solution(6234613447369685872)
XLA Ops:
  7.2 0.0 reduce-scatter.11.cloned.1.call-start
  7.2 0.7 convert_element_type.135
  7.9 0.7 fusion.36
  8.7 1.8 broadcast_multiply_fusion
  10.5 1.3 copy-done.1
  11.8 16.0 %fusion.10 = bf16[2,32,128,128]{3,2,1,0:T(8,128)(2,1)S(1)} fusion(bf16[2,32,128,128]{3,2,1,0:T(8,128)(2,1)S(1)} %broadcast_multiply_fusion, f32[128]{0:T(128)S(1)} %get-tuple-element.153, f32[128]{0:T(128)S(1)} %get-tuple-element.154, f32[128]{0:T(128)S(1)} %get-tuple-element.155, f32[128]{0:T(128)S(1)} %get-tuple-element.156, ...), kind=kLoop, calls=%fused_computation.50 | loop fusion | flops 28311552 | bytes 4198928 | tf_op jit(solution)/shard_map/convert_element_type | solution.py:69
  27.8 4.5 convolution_bitcast_fusion.1
  32.3 8.9 %copy.33 = f32[256,8192]{1,0:T(8,128)} copy(f32[256,8192]{0,1:T(8,128)} %convolution_bitcast_fusion.1) | data formatting | bytes 16777216
  41.2 0.2 reduce-scatter.13.cloned.1.call-start
  41.5 73.4 %reduce-scatter.11.cloned.1.call-done = f32[16,8192]{1,0:T(8,128)} async-done(((f32[256,8192]{1,0:T(8,128)}), f32[16,8192]{1,0:T(8,128)}) %reduce-scatter.11.cloned.1.call-update) | async-done | bytes 524304 | tf_op jit(solution)/shard_map/reduce_scatter | solution.py:75
  114.9 5.6 %convolution_bitcast_fusion = f32[256,8192]{0,1:T(8,128)} fusion(bf16[1,16,256]{2,1,0:T(8,128)(2,1)S(1)} %copy-done.7, f32[16,8192]{1,0:T(8,128)} %reduce-scatter.11.cloned.1.call-done, f32[16]{0:T(128)S(1)} %bitcast.133), kind=kOutput, calls=%fused_computation.27 | convolution fusion | flops 67895296 | bytes 8921152 | tf_op jit(solution)/shard_map/dot_general | solution.py:89
  120.6 8.9 %copy.35 = f32[256,8192]{1,0:T(8,128)} copy(f32[256,8192]{0,1:T(8,128)} %convolution_bitcast_fusion) | data formatting | bytes 16777216
  129.5 0.0 all-gather.9.cloned.1.call-start
  129.6 69.4 %reduce-scatter.13.cloned.1.call-done = f32[16,8192]{1,0:T(8,128)} async-done(((f32[256,8192]{1,0:T(8,128)}), f32[16,8192]{1,0:T(8,128)}) %reduce-scatter.13.cloned.1.call-update) | async-done | bytes 524304 | tf_op jit(solution)/shard_map/reduce_scatter | solution.py:88
  199.0 0.0 all-reduce.9.cloned.1.call-start
  199.0 0.8 convert.2
  199.9 32.1 %all-gather.9.cloned.1.call-done = f32[64,8192]{1,0:T(8,128)} async-done(((f32[16,8192]{1,0:T(8,128)}), f32[64,8192]{1,0:T(8,128)}) %all-gather.9.cloned.1.call-update) | async-done | bytes 2097168 | tf_op jit(solution)/shard_map/all_gather | solution.py:13
  232.0 4.9 while.14
  232.0 1.3 add_select_fusion.2
  233.3 1.2 add_select_fusion.2
  234.5 1.2 add_select_fusion.2
  235.7 1.2 add_select_fusion.2
  236.9 2.4 broadcast_select_fusion
  239.3 0.8 copy.39
  240.1 0.0 all-gather.5.cloned.1.call-start
  240.2 48.3 %all-reduce.9.cloned.1.call-done = (bf16[16,2,32,128]{3,2,1,0:T(8,128)(2,1)}, bf16[16,8192]{1,0:T(8,128)(2,1)}) async-done(((bf16[16,2,32,128]{3,2,1,0:T(8,128)(2,1)}, bf16[16,8192]{1,0:T(8,128)(2,1)}), (bf16[16,2,32,128]{3,2,1,0:T(8,128)(2,1)}, bf16[16,8192]{1,0:T(8,128)(2,1)})) %all-reduce.9.cloned.1.call-update) | async-done | bytes 524304 | tf_op jit(solution)/shard_map/psum | solution.py:26
  288.5 0.0 all-gather.7.cloned.1.call-start
  288.5 45.4 %all-gather.5.cloned.1.call-done = bf16[256,8192]{1,0:T(8,128)(2,1)} async-done(((bf16[16,8192]{1,0:T(8,128)(2,1)}), bf16[256,8192]{1,0:T(8,128)(2,1)}) %all-gather.5.cloned.1.call-update) | async-done | bytes 4194320 | tf_op jit(solution)/shard_map/all_gather | solution.py:108
  333.9 3.7 convert_reduce_fusion.1
  337.6 0.0 reduce-scatter.15.cloned.1.call-start
  337.6 40.8 %all-gather.7.cloned.1.call-done = bf16[256,8192]{1,0:T(8,128)(2,1)} async-done(((bf16[16,8192]{1,0:T(8,128)(2,1)}), bf16[256,8192]{1,0:T(8,128)(2,1)}) %all-gather.7.cloned.1.call-update) | async-done | bytes 4194320 | tf_op jit(solution)/shard_map/all_gather | solution.py:117
  378.4 16.1 %fusion.24 = (f32[128]{0:T(128)S(1)}, f32[128]{0:T(128)S(1)}, f32[128]{0:T(128)S(1)}, f32[128]{0:T(128)S(1)}, f32[128]{0:T(128)S(1)}, /*index=5*/f32[128]{0:T(12...) fusion(s32[]{:T(128)S(6)} %select_n.96, s32[]{:T(128)S(6)} %select_n.95, ...), kind=kOutput, calls=%fused_computation.64 | convolution fusion | flops 567278464 | bytes 8458768 | tf_op jit(solution)/shard_map/dot_general | solution.py:119
  394.5 16.2 %fusion.15 = f32[2,32,128,128]{3,2,1,0:T(8,128)S(1)} fusion(bf16[2,32,128,128]{3,2,1,0:T(8,128)(2,1)S(1)} %bitcast.127, s32[]{:T(128)S(6)} %select_n.96, s32[]{:T(128)S(6)} %select_n.95, s32[]{:T(128)S(6)} %select_n.94, s32[]{:T(128)S(6)} %select_n.93, f32[128]{0:T(128)S(1)} %get-tuple-element.153, f32[128]{0:T(128)S(1)} %get-tuple-element.154, ...), kind=kLoop, calls=%fused_computation.55 | loop fusion | flops 27262976 | bytes 6296080 | tf_op jit(solution)/shard_map/add | solution.py:138
  410.7 0.3 copy.37
  411.0 4.4 copy.50
  415.4 0.3 all-reduce.7.cloned.1.call-start
  415.7 0.6 copy-done.3
  416.3 0.2 convert_reduce_fusion
  416.5 3.4 fusion.26
  420.0 17.6 %all-reduce.2 = (f32[1,9,128]{2,1,0:T(8,128)S(1)}, f32[1,16]{1,0:T(1,128)}, f32[1,16,256]{2,1,0:T(8,128)}, f32[16]{0:T(128)}) all-reduce(f32[1,9,128]{2,1,0:T(8,128)S(1)} %bitcast.132, f32[1,16]{1,0:T(1,128)S(1)} %multiply_bitcast_fusion, f32[1,16,256]{2,1,0:T(8,128)S(1)} %fusion.26, ...), channel_id=1, replica_groups=mesh['section'=4,'dp'=4,'chan'=16] {'dp'}, use_global_device_ids=true, to_apply=%region_16.17 | all-reduce | flops 5280 | bytes 42240 | tf_op jit(solution)/shard_map/psum | solution.py:144
  437.7 0.6 copy.32
  438.3 4.5 fusion.25
  442.8 18.3 %reduce-scatter.15.cloned.1.call-done = f32[8,32768]{1,0:T(8,128)} async-done(((f32[32,32768]{1,0:T(8,128)}), f32[8,32768]{1,0:T(8,128)}) %reduce-scatter.15.cloned.1.call-update) | async-done | bytes 1048592
  461.1 1.4 copy.42
  462.5 1.0 fusion.27
  463.5 47.9 %all-reduce.7.cloned.1.call-done = f32[1,128,256]{2,1,0:T(8,128)} async-done(((f32[1,128,256]{2,1,0:T(8,128)}), f32[1,128,256]{2,1,0:T(8,128)}) %all-reduce.7.cloned.1.call-update) | async-done | bytes 131088 | tf_op jit(solution)/shard_map/psum | solution.py:144
  511.4 0.7 copy.60
  512.1 1.6 copy.61
  (37 shorter events, 0.3 us)
Async XLA Ops:
  7.2 20.7 %copy-start = (bf16[1,128,256]{2,1,0:T(8,128)(2,1)S(1)}, bf16[1,128,256]{2,1,0:T(8,128)(2,1)}, u32[]{:S(2)}) copy-start(bf16[1,128,256]{2,1,0:T(8,128)(2,1)} %param.17) | copy-start | bytes 196612
  7.2 107.7 %reduce-scatter.11.cloned.1.call-start = ((), (), s32[]{:S(2)}) async-start(), calls=%async_computation.7 | async-start | bytes 8912896 | tf_op jit(solution)/shard_map/reduce_scatter | solution.py:75
  10.5 1.4 copy-start.1
  41.2 73.7 %copy-start.7 = (bf16[1,16,256]{2,1,0:T(8,128)(2,1)S(1)}, bf16[1,16,256]{2,1,0:T(8,128)(2,1)}, u32[]{:S(2)}) copy-start(bf16[1,16,256]{2,1,0:T(8,128)(2,1)} %param.19) | copy-start | bytes 24580
  41.2 73.7 %copy-start.8 = (f32[1,16]{1,0:T(1,128)S(1)}, f32[1,16]{1,0:T(1,128)}, u32[]{:S(2)}) copy-start(f32[1,16]{1,0:T(1,128)} %param.18) | copy-start | bytes 196
  41.2 157.7 %reduce-scatter.13.cloned.1.call-start = ((), (), s32[]{:S(2)}) async-start(), calls=%async_computation.8 | async-start | bytes 8912896 | tf_op jit(solution)/shard_map/reduce_scatter | solution.py:88
  129.5 69.5 %copy-start.4 = (bf16[16,2,32,128]{3,2,1,0:T(8,128)(2,1)S(1)}, bf16[16,2,32,128]{3,2,1,0:T(8,128)(2,1)}, u32[]{:S(2)}) copy-start(bf16[16,2,32,128]{3,2,1,0:T(8,128)(2,1)} %param.21) | copy-start | bytes 786436
  129.5 70.4 %copy-start.6 = (s32[2,32,128]{2,1,0:T(8,128)S(1)}, s32[2,32,128]{2,1,0:T(8,128)}, u32[]{:S(2)}) copy-start(s32[2,32,128]{2,1,0:T(8,128)} %param.15) | copy-start | bytes 98308
  129.5 102.5 %all-gather.9.cloned.1.call-start = ((), (), s32[]{:S(2)}) async-start(), calls=%async_computation.6 | async-start | bytes 2621440 | tf_op jit(solution)/shard_map/all_gather | solution.py:13
  199.0 89.5 %all-reduce.9.cloned.1.call-start = ((), (), s32[]{:S(2)}) async-start(), calls=%async_computation.10 | async-start | bytes 1048576 | tf_op jit(solution)/shard_map/psum | solution.py:26
  199.9 37.0 %copy-start.9 = (f32[16]{0:T(128)S(1)}, f32[16]{0:T(128)}, u32[]{:S(2)}) copy-start(f32[16]{0:T(128)} %param.20) | copy-start | bytes 196
  232.0 101.9 %copy-start.2 = (f32[16,8192]{1,0:T(8,128)S(1)}, f32[16,8192]{1,0:T(8,128)}, u32[]{:S(2)}) copy-start(f32[16,8192]{1,0:T(8,128)} %reduce-scatter.11.cloned.1.call-done) | copy-start | bytes 1572868
  240.1 93.8 %all-gather.5.cloned.1.call-start = ((), (), s32[]{:S(2)}) async-start(), calls=%async_computation.3 | async-start | bytes 4456448 | tf_op jit(solution)/shard_map/all_gather | solution.py:108
  288.5 90.0 %all-gather.7.cloned.1.call-start = ((), (), s32[]{:S(2)}) async-start(), calls=%async_computation.4 | async-start | bytes 4456448 | tf_op jit(solution)/shard_map/all_gather | solution.py:117
  337.6 123.5 %reduce-scatter.15.cloned.1.call-start = ((), (), s32[]{:S(2)}) async-start(), calls=%async_computation.9 | async-start | bytes 5242880
  415.4 0.9 copy-start.3
  415.4 95.9 %all-reduce.7.cloned.1.call-start = ((), (), s32[]{:S(2)}) async-start(), calls=%async_computation.5 | async-start | bytes 262144 | tf_op jit(solution)/shard_map/psum | solution.py:144
  438.3 73.1 %copy-start.5 = (bf16[16,2,32,128]{3,2,1,0:T(8,128)(2,1)S(1)}, bf16[16,2,32,128]{3,2,1,0:T(8,128)(2,1)}, u32[]{:S(2)}) copy-start(bf16[16,2,32,128]{3,2,1,0:T(8,128)(2,1)} %get-tuple-element.217) | copy-start | bytes 786436
Sparse Core Ops, SparseCore 0:
  41.4 73.4 reduce-scatter.10
  129.6 69.2 reduce-scatter.12
  200.8 31.1 all-gather.8
  240.2 48.1 all-reduce.8
  290.1 43.7 all-gather.4
  337.7 40.6 all-gather.6
  415.5 45.4 reduce-scatter.14
  464.0 47.2 all-reduce.6
where the time goes:
time: 521 us; the launch traced here: 520 us
  waiting for transfers between devices  376 us (72%)
  other arithmetic  44.7 us (9%)
  matrix products  37.7 us (7%)
  local copies, waits for them, and re-layouts  29.6 us (6%)
  blocking collectives  17.6 us (3%)
  between operations  14.3 us (3%)
    reduce_scatter x1, waiting for transfers between devices, local(): lax.psum_scatter(lax.dot_general(columns, depth_rows, (((0,), (1,)), ((),...  73.4 us
    reduce_scatter x1, waiting for transfers between devices, local(): lax.psum_scatter(lax.dot_general(columns, branch_act, (((0,), (0,)), ((),...  69.4 us
    psum x1, waiting for transfers between devices, spread(): return lax.psum(kept, axis)  48.3 us
    psum x1, waiting for transfers between devices, local(): lax.psum((kernel_grad, weight_grad * scaling, pw_bias_grad, proj_grad * s...  47.9 us
    all_gather x1, waiting for transfers between devices, local(): shard_rows = lax.all_gather(out_grad, 'chan', axis=0, tiled=True)  45.4 us
    all_gather x1, waiting for transfers between devices, local(): shard_rows = lax.all_gather(pre_grad, 'chan', axis=0, tiled=True)  40.8 us
    all_gather x1, waiting for transfers between devices, prefix(): everything = lax.all_gather(shard, axis)  32.1 us
    unnamed x29, local copies, waits for them, and re-layouts  29.6 us
  transfers between devices with their start and end apart: 8, of which 8 were waited for; matrix products, arithmetic and copies ran while one was open for 2% of the time, Pallas kernels for 0%

commit v1 on v0

--- a/solution.py
+++ b/solution.py
@@ -6,6 +6,13 @@
 
 RATE = 6
 void_class = 19
+
+
+def all_by_exchange(x, axis, along):
+    size = lax.axis_size(axis)
+    parts = jnp.stack([x for _ in range(size)])
+    parts = lax.all_to_all(parts, axis, split_axis=0, concat_axis=0)
+    return jnp.concatenate(parts, axis=along)
 
 
 def prefix(shard, axis, combine, identity):
@@ -105,7 +112,7 @@
         spread(out_grad, "section", segments - 1),
     )
     proj_bias_grad = jnp.sum(out_grad.astype(jnp.float32), axis=1) * scaling
-    shard_rows = lax.all_gather(out_grad, "chan", axis=0, tiled=True)
+    shard_rows = all_by_exchange(out_grad, "chan", 0)
     act_grad = jnp.dot(proj_local, shard_rows, preferred_element_type=jnp.float32)
     piece_grad = lax.dot_general(
         branch_act, shard_rows, (((1,), (1,)), ((), ())), preferred_element_type=jnp.float32

time: 521 us -> 579 us (1.11)
  blocking collectives: 17.6 us -> 119 us
  waiting for transfers between devices: 376 us -> 330 us
    all_to_all x0 -> x1, blocking collectives: none -> 102 us  [all_by_exchange(): parts = lax.all_to_all(parts, axis, split_axis=0, concat_axis=0)]
    all_gather x1 -> x0, waiting for transfers between devices: 45.4 us -> none  [local(): shard_rows = lax.all_gather(out_grad, 'chan', axis=0, tiled=True)]
    unnamed x29 -> x33, local copies, waits for them, and re-layouts: 29.6 us -> 31.5 us
    unnamed x9 -> x8, waiting for transfers between devices: 18.4 us -> 18.4 us
  transfers between devices with their start and end apart: 8 -> 7, of which waited for: 8 -> 7; matrix products, arithmetic and copies ran while one was open for 2% -> 2% of each run, Pallas kernels for 0% -> 0%
where the time goes in v1:
time: 579 us; the launch traced here: 578 us
  waiting for transfers between devices  330 us (57%)
  blocking collectives  119 us (21%)
  other arithmetic  44.5 us (8%)
  matrix products  35.6 us (6%)
  local copies, waits for them, and re-layouts  33 us (6%)
  between operations  14.3 us (2%)
    all_to_all x1, blocking collectives, all_by_exchange(): parts = lax.all_to_all(parts, axis, split_axis=0, concat_axis=0)  102 us
    reduce_scatter x1, waiting for transfers between devices, local(): lax.psum_scatter(lax.dot_general(columns, depth_rows, (((0,), (1,)), ((),...  73.4 us
    reduce_scatter x1, waiting for transfers between devices, local(): lax.psum_scatter(lax.dot_general(columns, branch_act, (((0,), (0,)), ((),...  69.4 us
    psum x1, waiting for transfers between devices, spread(): return lax.psum(kept, axis)  48.3 us
    psum x1, waiting for transfers between devices, local(): lax.psum((kernel_grad, weight_grad * scaling, pw_bias_grad, proj_grad * s...  47.9 us
    all_gather x1, waiting for transfers between devices, local(): shard_rows = lax.all_gather(pre_grad, 'chan', axis=0, tiled=True)  40.9 us
    all_gather x1, waiting for transfers between devices, prefix(): everything = lax.all_gather(shard, axis)  32.1 us
    unnamed x33, local copies, waits for them, and re-layouts  31.5 us
  transfers between devices with their start and end apart: 7, of which 7 were waited for; matrix products, arithmetic and copies ran while one was open for 2% of the time, Pallas kernels for 0%

profile of v1, /device:TPU:2, one launch (start us, length us, event | category | flops | bytes accessed | tf_op | source)
XLA Modules:
  0.0 577.9 jit_solution(3494260360236183728)
XLA Ops:
  7.2 0.7 convert_element_type.135
  7.9 0.7 fusion.36
  8.7 1.8 broadcast_multiply_fusion
  10.5 1.3 copy-done.2
  11.8 16.0 %fusion.10 = bf16[2,32,128,128]{3,2,1,0:T(8,128)(2,1)S(1)} fusion(bf16[2,32,128,128]{3,2,1,0:T(8,128)(2,1)S(1)} %broadcast_multiply_fusion, f32[128]{0:T(128)S(1)} %get-tuple-element.153, f32[128]{0:T(128)S(1)} %get-tuple-element.154, f32[128]{0:T(128)S(1)} %get-tuple-element.155, f32[128]{0:T(128)S(1)} %get-tuple-element.156, ...), kind=kLoop, calls=%fused_computation.50 | loop fusion | flops 28311552 | bytes 4198928 | tf_op jit(solution)/shard_map/convert_element_type | solution.py:76
  27.8 4.5 convolution_bitcast_fusion.1
  32.3 8.9 %copy.35 = f32[256,8192]{1,0:T(8,128)} copy(f32[256,8192]{0,1:T(8,128)} %convolution_bitcast_fusion.1) | data formatting | bytes 16777216
  41.2 0.2 reduce-scatter.13.cloned.1.call-start
  41.5 73.4 %reduce-scatter.11.cloned.1.call-done = f32[16,8192]{1,0:T(8,128)} async-done(((f32[256,8192]{1,0:T(8,128)}), f32[16,8192]{1,0:T(8,128)}) %reduce-scatter.11.cloned.1.call-update) | async-done | bytes 524304 | tf_op jit(solution)/shard_map/reduce_scatter | solution.py:82
  114.9 5.6 convolution_bitcast_fusion
  120.6 8.9 %copy.37 = f32[256,8192]{1,0:T(8,128)} copy(f32[256,8192]{0,1:T(8,128)} %convolution_bitcast_fusion) | data formatting | bytes 16777216
  129.5 0.0 all-gather.6.cloned.1.call-start
  129.6 69.4 %reduce-scatter.13.cloned.1.call-done = f32[16,8192]{1,0:T(8,128)} async-done(((f32[256,8192]{1,0:T(8,128)}), f32[16,8192]{1,0:T(8,128)}) %reduce-scatter.13.cloned.1.call-update) | async-done | bytes 524304 | tf_op jit(solution)/shard_map/reduce_scatter | solution.py:95
  199.0 0.0 all-reduce.9.cloned.1.call-start
  199.0 0.8 convert.2
  199.9 32.1 %all-gather.6.cloned.1.call-done = f32[64,8192]{1,0:T(8,128)} async-done(((f32[16,8192]{1,0:T(8,128)}), f32[64,8192]{1,0:T(8,128)}) %all-gather.6.cloned.1.call-update) | async-done | bytes 2097168 | tf_op jit(solution)/shard_map/all_gather | solution.py:20
  232.0 4.9 while.14
  232.0 1.2 add_select_fusion.2
  233.2 1.2 add_select_fusion.2
  234.4 1.2 add_select_fusion.2
  235.7 1.2 add_select_fusion.2
  236.9 2.2 broadcast_select_fusion
  239.1 0.8 copy.41
  239.9 0.0 all-gather.4.cloned.1.call-start
  239.9 48.3 %all-reduce.9.cloned.1.call-done = (bf16[16,2,32,128]{3,2,1,0:T(8,128)(2,1)}, bf16[16,8192]{1,0:T(8,128)(2,1)}) async-done(((bf16[16,2,32,128]{3,2,1,0:T(8,128)(2,1)}, bf16[16,8192]{1,0:T(8,128)(2,1)}), (bf16[16,2,32,128]{3,2,1,0:T(8,128)(2,1)}, bf16[16,8192]{1,0:T(8,128)(2,1)})) %all-reduce.9.cloned.1.call-update) | async-done | bytes 524304 | tf_op jit(solution)/shard_map/psum | solution.py:33
  288.2 1.4 stack.4
  289.6 101.7 %all_to_all.5 = bf16[16,16,8192]{2,1,0:T(8,128)(2,1)S(1)} all-to-all(bf16[16,16,8192]{2,1,0:T(8,128)(2,1)S(1)} %stack.4), channel_id=1, replica_groups=mesh['section'=4,'dp'=4,'chan'=16] {'chan'}, dimensions={0} | all-to-all | bytes 8388608 | tf_op jit(solution)/shard_map/all_to_all | solution.py:14
  391.4 1.9 copy-done.1
  393.3 1.5 convert_reduce_fusion.1
  394.8 0.0 reduce-scatter.15.cloned.1.call-start
  394.9 40.9 %all-gather.4.cloned.1.call-done = bf16[256,8192]{1,0:T(8,128)(2,1)} async-done(((bf16[16,8192]{1,0:T(8,128)(2,1)}), bf16[256,8192]{1,0:T(8,128)(2,1)}) %all-gather.4.cloned.1.call-update) | async-done | bytes 4194320 | tf_op jit(solution)/shard_map/all_gather | solution.py:124
  435.8 16.1 %fusion.24 = (f32[128]{0:T(128)S(1)}, f32[128]{0:T(128)S(1)}, f32[128]{0:T(128)S(1)}, f32[128]{0:T(128)S(1)}, f32[128]{0:T(128)S(1)}, /*index=5*/f32[128]{0:T(12...) fusion(s32[]{:T(128)S(6)} %select_n.96, s32[]{:T(128)S(6)} %select_n.95, ...), kind=kOutput, calls=%fused_computation.64 | convolution fusion | flops 567278464 | bytes 8458768 | tf_op jit(solution)/shard_map/dot_general | solution.py:126
  451.9 16.2 %fusion.15 = f32[2,32,128,128]{3,2,1,0:T(8,128)S(1)} fusion(bf16[2,32,128,128]{3,2,1,0:T(8,128)(2,1)S(1)} %bitcast.130, s32[]{:T(128)S(6)} %select_n.96, s32[]{:T(128)S(6)} %select_n.95, s32[]{:T(128)S(6)} %select_n.94, s32[]{:T(128)S(6)} %select_n.93, f32[128]{0:T(128)S(1)} %get-tuple-element.153, f32[128]{0:T(128)S(1)} %get-tuple-element.154, ...), kind=kLoop, calls=%fused_computation.55 | loop fusion | flops 27262976 | bytes 6296080 | tf_op jit(solution)/shard_map/add | solution.py:145
  468.1 0.3 copy.39
  468.4 4.4 copy.52
  472.8 0.3 all-reduce.7.cloned.1.call-start
  473.1 0.6 copy-done.5
  473.7 0.2 convert_reduce_fusion
  473.9 3.4 fusion.26
  477.4 17.6 %all-reduce.2 = (f32[1,9,128]{2,1,0:T(8,128)S(1)}, f32[1,16]{1,0:T(1,128)}, f32[1,16,256]{2,1,0:T(8,128)}, f32[16]{0:T(128)}) all-reduce(f32[1,9,128]{2,1,0:T(8,128)S(1)} %bitcast.135, f32[1,16]{1,0:T(1,128)S(1)} %multiply_bitcast_fusion, f32[1,16,256]{2,1,0:T(8,128)S(1)} %fusion.26, ...), channel_id=1, replica_groups=mesh['section'=4,'dp'=4,'chan'=16] {'dp'}, use_global_device_ids=true, to_apply=%region_16.17 | all-reduce | flops 5280 | bytes 42240 | tf_op jit(solution)/shard_map/psum | solution.py:151
  495.1 0.6 copy.34
  495.6 4.5 fusion.25
  500.2 18.3 %reduce-scatter.15.cloned.1.call-done = f32[8,32768]{1,0:T(8,128)} async-done(((f32[32,32768]{1,0:T(8,128)}), f32[8,32768]{1,0:T(8,128)}) %reduce-scatter.15.cloned.1.call-update) | async-done | bytes 1048592
  518.4 1.4 copy.44
  519.9 1.0 fusion.27
  520.8 47.9 %all-reduce.7.cloned.1.call-done = f32[1,128,256]{2,1,0:T(8,128)} async-done(((f32[1,128,256]{2,1,0:T(8,128)}), f32[1,128,256]{2,1,0:T(8,128)}) %all-reduce.7.cloned.1.call-update) | async-done | bytes 131088 | tf_op jit(solution)/shard_map/psum | solution.py:151
  568.7 0.7 copy.62
  569.4 1.6 copy.63
  (40 shorter events, 0.3 us)
Async XLA Ops:
  7.2 20.7 %copy-start = (bf16[1,128,256]{2,1,0:T(8,128)(2,1)S(1)}, bf16[1,128,256]{2,1,0:T(8,128)(2,1)}, u32[]{:S(2)}) copy-start(bf16[1,128,256]{2,1,0:T(8,128)(2,1)} %param.17) | copy-start | bytes 196612
  7.2 107.7 %reduce-scatter.11.cloned.1.call-start = ((), (), s32[]{:S(2)}) async-start(), calls=%async_computation.7 | async-start | bytes 8912896 | tf_op jit(solution)/shard_map/reduce_scatter | solution.py:82
  10.5 1.4 copy-start.2
  41.2 73.7 %copy-start.9 = (bf16[1,16,256]{2,1,0:T(8,128)(2,1)S(1)}, bf16[1,16,256]{2,1,0:T(8,128)(2,1)}, u32[]{:S(2)}) copy-start(bf16[1,16,256]{2,1,0:T(8,128)(2,1)} %param.19) | copy-start | bytes 24580
  41.2 73.7 %copy-start.10 = (f32[1,16]{1,0:T(1,128)S(1)}, f32[1,16]{1,0:T(1,128)}, u32[]{:S(2)}) copy-start(f32[1,16]{1,0:T(1,128)} %param.18) | copy-start | bytes 196
  41.2 157.7 %reduce-scatter.13.cloned.1.call-start = ((), (), s32[]{:S(2)}) async-start(), calls=%async_computation.8 | async-start | bytes 8912896 | tf_op jit(solution)/shard_map/reduce_scatter | solution.py:95
  129.5 69.5 %copy-start.6 = (bf16[16,2,32,128]{3,2,1,0:T(8,128)(2,1)S(1)}, bf16[16,2,32,128]{3,2,1,0:T(8,128)(2,1)}, u32[]{:S(2)}) copy-start(bf16[16,2,32,128]{3,2,1,0:T(8,128)(2,1)} %param.21) | copy-start | bytes 786436
  129.5 70.4 %copy-start.8 = (s32[2,32,128]{2,1,0:T(8,128)S(1)}, s32[2,32,128]{2,1,0:T(8,128)}, u32[]{:S(2)}) copy-start(s32[2,32,128]{2,1,0:T(8,128)} %param.15) | copy-start | bytes 98308
  129.5 102.5 %all-gather.6.cloned.1.call-start = ((), (), s32[]{:S(2)}) async-start(), calls=%async_computation.6 | async-start | bytes 2621440 | tf_op jit(solution)/shard_map/all_gather | solution.py:20
  199.0 89.3 %all-reduce.9.cloned.1.call-start = ((), (), s32[]{:S(2)}) async-start(), calls=%async_computation.10 | async-start | bytes 1048576 | tf_op jit(solution)/shard_map/psum | solution.py:33
  199.9 37.0 %copy-start.4 = (f32[16,8192]{1,0:T(8,128)S(1)}, f32[16,8192]{1,0:T(8,128)}, u32[]{:S(2)}) copy-start(f32[16,8192]{1,0:T(8,128)} %reduce-scatter.13.cloned.1.call-done) | copy-start | bytes 1572868
  199.9 37.0 %copy-start.11 = (f32[16]{0:T(128)S(1)}, f32[16]{0:T(128)}, u32[]{:S(2)}) copy-start(f32[16]{0:T(128)} %param.20) | copy-start | bytes 196
  239.9 195.9 %all-gather.4.cloned.1.call-start = ((), (), s32[]{:S(2)}) async-start(), calls=%async_computation.4 | async-start | bytes 4456448 | tf_op jit(solution)/shard_map/all_gather | solution.py:124
  289.6 103.7 %copy-start.3 = (f32[16,8192]{1,0:T(8,128)S(1)}, f32[16,8192]{1,0:T(8,128)}, u32[]{:S(2)}) copy-start(f32[16,8192]{1,0:T(8,128)} %reduce-scatter.11.cloned.1.call-done) | copy-start | bytes 1572868
  391.4 1.9 copy-start.1
  394.8 123.6 %reduce-scatter.15.cloned.1.call-start = ((), (), s32[]{:S(2)}) async-start(), calls=%async_computation.9 | async-start | bytes 5242880
  472.8 0.9 copy-start.5
  472.8 95.9 %all-reduce.7.cloned.1.call-start = ((), (), s32[]{:S(2)}) async-start(), calls=%async_computation.5 | async-start | bytes 262144 | tf_op jit(solution)/shard_map/psum | solution.py:151
  495.6 73.1 %copy-start.7 = (bf16[16,2,32,128]{3,2,1,0:T(8,128)(2,1)S(1)}, bf16[16,2,32,128]{3,2,1,0:T(8,128)(2,1)}, u32[]{:S(2)}) copy-start(bf16[16,2,32,128]{3,2,1,0:T(8,128)(2,1)} %get-tuple-element.217) | copy-start | bytes 786436
Sparse Core Ops, SparseCore 0:
  41.4 73.4 reduce-scatter.10
  129.6 69.2 reduce-scatter.12
  200.8 31.1 all-gather.5
  240.0 48.1 all-reduce.8
  394.9 40.8 all-gather.3
  472.9 45.4 reduce-scatter.14
  521.4 47.2 all-reduce.6
